TPU v7x, 32 devices: a whole 2x2x4 slice. The times are simulated.
32 devices in a mesh: blk: 8 (over y, x, core), cross: 4 (over z).
Axes of the slice: x: 2, y: 2, z: 4, core: 2. Of those that a mesh axis runs over, the one named last changes fastest.
Arguments:
- receiver_spectra: float32 [4096, 2, 1024], P(('blk', 'cross')), may hold values from -400 to 400
- source_spectra: float32 [4096, 2, 1024], P(('blk', 'cross')), may hold values from -400 to 400
- quality: int32 [4096], P(('blk', 'cross')), may hold values 0 or 1
- slot_order: int32 [32, 128], P(('blk', 'cross')), may hold values from 0 to 127, each once within a row
- owners: int32 [2, 8], replicated, may hold values from 0 to 3
Outputs:
- correlations: bfloat16 [2, 8, 4, 128, 128, 256], P(None, 'blk', 'cross')
Inputs may be any that keep to these rules, and one draw needn't show every extreme that they name: `slot_order`: each row is a permutation of 0 to 127.
All inputs are finite; a program needn't handle non-finite values. No bound on the sum of `quality` on one device may be relied on, other than what follows from the above.
Results may differ from a plain program's by a relative error of at most 0.0056.
Values sent between devices are 32-bit elements; how exact they have to be, the bound alone decides.
A program may use at most 128 MiB of HBM per device.

v0:
```python
import math
import jax
import jax.numpy as jnp
from jax import lax
from jax.sharding import PartitionSpec as P

L = 256
STEPS = 2


def passed_along(value, axis, steps):
    count = lax.axis_size(axis)
    pairs = [(source, (source + steps) % count) for source in range(count)]
    return lax.ppermute(value, axis, pairs)


def lag_tables(bins, lags):
    bin_index = jnp.arange(bins, dtype=jnp.int32)
    odd_index = 2 * jnp.arange(lags // 2, dtype=jnp.int32) + 1
    phase_turns = jnp.mod(bin_index[:, None] * odd_index[None, :], 4 * bins).astype(jnp.float32)
    phase_angle = phase_turns * (math.pi / (2 * bins))
    cos_table = (jnp.cos(phase_angle) / bins).astype(jnp.bfloat16)
    sin_table = (-jnp.sin(phase_angle) / bins).astype(jnp.bfloat16)
    return (cos_table, sin_table)


def whiten(spectra):
    mean_power = jnp.mean(spectra * spectra, axis=(1, 2), keepdims=True)
    return spectra * lax.rsqrt(mean_power + 1e-06)


def correlate(panel_spec, slab_spec, cos_table, sin_table):
    npanel = panel_spec.shape[0]
    nslab = slab_spec.shape[0]
    width = math.gcd(npanel, 16)
    blocks = panel_spec.reshape(npanel // width, width, 2, panel_spec.shape[2])

    def one_block(source):
        inphase = (
            source[:, None, 0, :] * slab_spec[None, :, 0, :]
            + source[:, None, 1, :] * slab_spec[None, :, 1, :]
        )
        quadrature = (
            source[:, None, 1, :] * slab_spec[None, :, 0, :]
            - source[:, None, 0, :] * slab_spec[None, :, 1, :]
        )
        inphase = inphase.astype(jnp.bfloat16).reshape(width * nslab, -1)
        quadrature = quadrature.astype(jnp.bfloat16).reshape(width * nslab, -1)
        even = jnp.dot(inphase, cos_table, preferred_element_type=jnp.float32)
        odd = jnp.dot(quadrature, sin_table, preferred_element_type=jnp.float32)
        joined = jnp.concatenate([even + odd, even - odd], axis=-1).astype(jnp.bfloat16)
        return joined.reshape(width, nslab, -1)

    lagged = lax.map(one_block, blocks)
    return lagged.reshape(npanel, nslab, lagged.shape[-1])


def local(receiver_spectra, source_spectra, quality, slot_order, owners):
    bins = receiver_spectra.shape[2]
    npanel = source_spectra.shape[0]
    cos_table, sin_table = lag_tables(bins, L)
    kept = quality.astype(jnp.float32)[:, None, None]
    receivers = whiten(receiver_spectra) * kept
    receivers = jnp.take(receivers, slot_order[0], axis=0)
    sources = whiten(source_spectra)
    block_index = lax.axis_index("blk")
    my_owners = lax.dynamic_index_in_dim(owners, block_index, 1, keepdims=False)
    every_panel = lax.all_gather(sources, "cross", axis=0, tiled=True)
    moving = receivers
    results = []
    for loop_step in range(STEPS):
        if loop_step > 0:
            moving = passed_along(moving, "blk", 1)
        owner_index = my_owners[loop_step]
        panel_spec = lax.dynamic_slice_in_dim(every_panel, owner_index * npanel, npanel, 0)
        results.append(correlate(panel_spec, moving, cos_table, sin_table))
    return jnp.stack(results)[:, None, None]


def solution(mesh):
    placed = (
        P(("blk", "cross"), None, None),
        P(("blk", "cross"), None, None),
        P(("blk", "cross")),
        P(("blk", "cross"), None),
        P(),
    )
    return jax.shard_map(
        local,
        mesh=mesh,
        in_specs=placed,
        out_specs=P(None, "blk", "cross", None, None, None),
        check_vma=False,
    )
```

profile of v0, /device:TPU:0, one launch (start us, length us, event | category | flops | bytes accessed | tf_op | source)
XLA Modules:
  0.0 305.8 jit_solution(16467009084390342149)
XLA Ops:
  6.5 2.3 multiply_reduce_fusion.1
  8.8 2.6 broadcast_multiply_fusion
  12.8 2.3 multiply_reduce_fusion
  15.1 1.7 multiply_multiply_fusion
  16.8 1.7 gather_fusion
  21.7 73.5 %all-gather.2.cloned.1.call-done = f32[512,2,1024]{2,1,0:T(2,128)} async-done(((f32[128,2,1024]{2,1,0:T(2,128)}), f32[512,2,1024]{2,1,0:T(2,128)}) %all-gather.2.cloned.1.call-update) | async-done | bytes 4194320 | tf_op jit(solution)/shard_map/all_gather | solution.py:68
  95.1 3.2 %constant_dynamic-slice_fusion.1 = (f32[128,2,1024]{2,1,0:T(2,128)S(1)}, f32[128,2,1024]{2,1,0:T(2,128)}) fusion(f32[512,2,1024]{2,1,0:T(2,128)} %all-gather.2.cloned.1.call-done, s32[]{:T(128)S(6)} %select_n.44, s32[]{:T(128)S(6)} %select_n.49), kind=kLoop, calls=%fused_computation.86 | loop fusion | bytes 4194312 | tf_op jit(solution)/shard_map/dynamic_slice | solution.py:75
  98.4 4.3 %broadcast.91.clone = bf16[8,16,128,256]{3,2,1,0:T(8,128)(2,1)} broadcast(bf16[]{:T(256)} %constant.66.clone.1), dimensions={} | broadcast | bytes 8388610 | tf_op jit(solution)/shard_map/broadcast.6
  102.6 92.7 %while.25 = (s32[]{:T(128)}, bf16[8,16,128,256]{3,2,1,0:T(8,128)(2,1)}, f32[8,16,2,1024]{3,2,1,0:T(2,128)}, f32[128,2,1024]{2,1,0:T(2,128)S(1)}, s32[128]{0:T(128)S(1)}, /*index=5*/s32[]{:T(128)}) while((s32[]{:T(128)}, bf16[8,16,128,256]{3,2,1,0:T(8,128)(2,1)}, f32[8,16,2,1024]{3,2,1,0:T(2,128)}, ...), condition=%wide.region_5.6_spmd.clone.clone, body=%wide.region_4.5_spmd.clone.clone.sunk | while | flops 1097990144 | bytes 28181588 | solution.py:54
  104.7 2.7 subtract_convert_fusion.7
  107.4 2.9 fusion.81
  110.3 2.8 add_convert_fusion.7
  116.3 2.7 subtract_convert_fusion.7
  119.0 2.9 fusion.81
  121.9 2.8 add_convert_fusion.7
  127.9 2.7 subtract_convert_fusion.7
  130.6 2.9 fusion.81
  133.4 2.8 add_convert_fusion.7
  139.5 2.7 subtract_convert_fusion.7
  142.1 2.9 fusion.81
  145.0 2.8 add_convert_fusion.7
  151.1 2.7 subtract_convert_fusion.7
  153.7 2.9 fusion.81
  156.6 2.8 add_convert_fusion.7
  162.6 2.7 subtract_convert_fusion.7
  165.3 2.9 fusion.81
  168.2 2.8 add_convert_fusion.7
  171.0 1.2 maximum_dynamic-update-slice_fusion.5
  174.2 2.7 subtract_convert_fusion.7
  176.9 2.9 fusion.81
  179.8 2.8 add_convert_fusion.7
  185.8 2.7 subtract_convert_fusion.7
  188.5 2.9 fusion.81
  191.4 2.8 add_convert_fusion.7
  194.2 1.2 maximum_dynamic-update-slice_fusion.5
  195.4 4.3 %broadcast.91.clone.1 = bf16[8,16,128,256]{3,2,1,0:T(8,128)(2,1)} broadcast(bf16[]{:T(256)} %constant.66.clone.1), dimensions={} | broadcast | bytes 8388610 | tf_op jit(solution)/shard_map/broadcast.6
  199.7 85.5 %while.24 = (s32[]{:T(128)}, bf16[8,16,128,256]{3,2,1,0:T(8,128)(2,1)}, f32[8,16,2,1024]{3,2,1,0:T(2,128)S(1)}, f32[128,2,1024]{2,1,0:T(2,128)S(1)}, s32[128]{0:T(128)S(1)}, /*index=5*/s32[]{:T(128)}) while((s32[]{:T(128)}, bf16[8,16,128,256]{3,2,1,0:T(8,128)(2,1)}, f32[8,16,2,1024]{3,2,1,0:T(2,128)S(1)}, ...), condition=%wide.region_3.4_spmd.clone.clone, body=%wide.region_2.3_spmd.clone.clone.sunk | while | flops 1097990144 | bytes 28181588 | solution.py:54
  200.8 2.7 subtract_convert_fusion.6
  203.5 2.9 fusion.76
  206.4 2.8 add_convert_fusion.6
  209.2 1.2 maximum_dynamic-update-slice_fusion.4
  211.6 2.7 subtract_convert_fusion.6
  214.3 2.9 fusion.76
  217.1 2.8 add_convert_fusion.6
  222.3 2.7 subtract_convert_fusion.6
  224.9 2.9 fusion.76
  227.8 2.8 add_convert_fusion.6
  232.9 2.7 subtract_convert_fusion.6
  235.6 2.9 fusion.76
  238.5 2.8 add_convert_fusion.6
  243.6 2.7 subtract_convert_fusion.6
  246.3 2.9 fusion.76
  249.2 2.8 add_convert_fusion.6
  252.0 1.2 maximum_dynamic-update-slice_fusion.4
  254.4 2.7 subtract_convert_fusion.6
  257.0 2.9 fusion.76
  259.9 2.8 add_convert_fusion.6
  265.0 2.7 subtract_convert_fusion.6
  267.7 2.9 fusion.76
  270.5 2.8 add_convert_fusion.6
  275.7 2.7 subtract_convert_fusion.6
  278.4 2.9 fusion.76
  281.2 2.8 add_convert_fusion.6
  285.2 13.8 %maximum_bitcast_fusion = bf16[2,1,1,128,128,256]{5,4,3,2,1,0:T(8,128)(2,1)} fusion(bf16[1,128,128,256]{3,2,1,0:T(8,128)(2,1)} %bitcast.87, bf16[1,128,128,256]{3,2,1,0:T(8,128)(2,1)} %bitcast.86), kind=kLoop, calls=%fused_computation.75 | loop fusion | flops 8388608 | bytes 33554432 | tf_op jit(solution)/shard_map/broadcast_in_dim | solution.py:77
  (112 shorter events, 42.5 us)
Async XLA Ops:
  6.5 13.2 %copy-start = (s32[2,8]{1,0:T(2,128)S(1)}, s32[2,8]{1,0:T(2,128)}, u32[]{:S(2)}) copy-start(s32[2,8]{1,0:T(2,128)} %param.13) | copy-start | bytes 196
  6.5 11.9 %copy-start.2 = (s32[1,128]{1,0:T(1,128)S(1)}, s32[1,128]{1,0:T(1,128)}, u32[]{:S(2)}) copy-start(s32[1,128]{1,0:T(1,128)} %param.12) | copy-start | bytes 1540
  6.5 88.6 %all-gather.2.cloned.1.call-start = ((), (), s32[]{:S(2)}) async-start(), calls=%async_computation | async-start | bytes 5242880 | tf_op jit(solution)/shard_map/all_gather | solution.py:68
  19.0 79.3 %collective-permute-start = (f32[128,2,1024]{2,1,0:T(2,128)S(1)}, f32[128,2,1024]{2,1,0:T(2,128)S(1)}, u32[]{:S(2)}, u32[]{:S(2)}) collective-permute-start(f32[128,2,1024]{2,1,0:T(2,128)S(1)} %broadcast_select_fusion), channel_id=1, source_target_pairs={{0,4},{4,8},{8,12},{12,16},{16,20},{20,24},{24,28},{28,0},{1,5},{5... | collective-permute-start | bytes 3145736 | tf_op jit(solution)/shard_map/ppermute | solution.py:14
  285.2 13.8 %copy-start.1 = (s32[2,8]{1,0:T(2,128)S(1)}, s32[2,8]{1,0:T(2,128)}, u32[]{:S(2)}) copy-start(s32[2,8]{1,0:T(2,128)} %param.13) | copy-start | bytes 196
Sparse Core Ops, SparseCore 0:
  11.6 83.4 all-gather.1
where the time goes:
time: 306 us
  matrix products  90.8 us (30%)
  other arithmetic  85.6 us (28%)
  waiting for transfers between devices  73.5 us (24%)
  local copies, waits for them, and re-layouts  39.7 us (13%)
  between operations  14.7 us (5%)
    all_gather x1, waiting for transfers between devices, local(): every_panel = lax.all_gather(sources, 'cross', axis=0, tiled=True)  73.5 us
    dot_general x16, matrix products, one_block(): odd = jnp.dot(quadrature, sin_table, preferred_element_type=jnp.float32)  45.8 us
    dot_general x16, matrix products, one_block(): even = jnp.dot(inphase, cos_table, preferred_element_type=jnp.float32)  45 us
    convert_element_type x16, other arithmetic, one_block(): quadrature = quadrature.astype(jnp.bfloat16).reshape(width * nslab, -1)  42.7 us
    dynamic_update_slice x16, other arithmetic, correlate(): lagged = lax.map(one_block, blocks)  18.4 us
    broadcast_in_dim x1, other arithmetic, local(): return jnp.stack(results)[:, None, None]  13.8 us
    slice x16, local copies, waits for them, and re-layouts, one_block(): slab_spec[None, :, 0, :]  13 us
    another operation x2, local copies, waits for them, and re-layouts  8.57 us
  transfers between devices with their start and end apart: 2, of which 1 were waited for; matrix products, arithmetic and copies ran while one was open for 4% of the time, Pallas kernels for 0%

commit v1 on v0

--- a/solution.py
+++ b/solution.py
@@ -6,6 +6,12 @@
 
 L = 256
 STEPS = 2
+
+
+def in_order(blocks, dim):
+    shape = list(blocks.shape[1:])
+    shape[dim] *= blocks.shape[0]
+    return jnp.moveaxis(blocks, 0, dim).reshape(shape)
 
 
 def passed_along(value, axis, steps):
@@ -65,7 +71,19 @@
     sources = whiten(source_spectra)
     block_index = lax.axis_index("blk")
     my_owners = lax.dynamic_index_in_dim(owners, block_index, 1, keepdims=False)
-    every_panel = lax.all_gather(sources, "cross", axis=0, tiled=True)
+    count_2 = lax.axis_size("cross")
+    pairs_2 = [(i, (i + 1) % count_2) for i in range(count_2)]
+    back = [(b, a) for a, b in pairs_2]
+    lower, upper = ([], [])
+    for turn in range(count_2 - 1):
+        if turn % 2 == 0:
+            lower.append(lax.ppermute(lower[-1] if lower else sources, "cross", pairs_2))
+        else:
+            upper.append(lax.ppermute(upper[-1] if upper else sources, "cross", back))
+    blocks_2 = jnp.stack([*lower[::-1], sources, *upper])
+    shift = lax.axis_index("cross") - len(lower)
+    blocks_2 = blocks_2[(jnp.arange(count_2) - shift) % count_2]
+    every_panel = in_order(blocks_2, 0)
     moving = receivers
     results = []
     for loop_step in range(STEPS):

time: 306 us -> 300 us (0.980)
  between operations: 14.7 us -> 1.46 us
  waiting for transfers between devices: 73.5 us -> 60.5 us
  local copies, waits for them, and re-layouts: 39.7 us -> 48.1 us
  starting transfers between devices: 0.73 us -> 6.76 us
  other arithmetic: 85.6 us -> 91.2 us
    all_gather x1 -> x0, waiting for transfers between devices: 73.5 us -> none  [local(): every_panel = lax.all_gather(sources, 'cross', axis=0, tiled=True)]
    ppermute x0 -> x3, waiting for transfers between devices: none -> 60.5 us  [the longest x2 60.5 us: local(): lax.ppermute(lower[-1] if lower else sources, 'cross', pairs_2)]
    gather x0 -> x1, local copies, waits for them, and re-layouts: none -> 8.36 us  [local(): blocks_2 = blocks_2[(jnp.arange(count_2) - shift) % count_2]]
    ppermute x0 -> x3, starting transfers between devices: none -> 6.7 us  [the longest x1 5.08 us: local(): upper.append(lax.ppermute(upper[-1] if upper else sources, 'cross', back))]
    another operation x0 -> x2, other arithmetic: none -> 5.63 us  [local(): blocks_2 = jnp.stack([*lower[::-1], sources, *upper])]
  transfers between devices with their start and end apart: 2 -> 4, of which waited for: 1 -> 2; matrix products, arithmetic and copies ran while one was open for 4% -> 8% of each run, Pallas kernels for 0% -> 0%
where the time goes in v1:
time: 300 us
  other arithmetic  91.2 us (30%)
  matrix products  90.8 us (30%)
  waiting for transfers between devices  60.5 us (20%)
  local copies, waits for them, and re-layouts  48.1 us (16%)
  starting transfers between devices  6.76 us (2%)
    ppermute x2, waiting for transfers between devices, local(): lax.ppermute(lower[-1] if lower else sources, 'cross', pairs_2)  60.5 us
    dot_general x16, matrix products, one_block(): odd = jnp.dot(quadrature, sin_table, preferred_element_type=jnp.float32)  45.8 us
    dot_general x16, matrix products, one_block(): even = jnp.dot(inphase, cos_table, preferred_element_type=jnp.float32)  45 us
    convert_element_type x16, other arithmetic, one_block(): quadrature = quadrature.astype(jnp.bfloat16).reshape(width * nslab, -1)  42.6 us
    dynamic_update_slice x16, other arithmetic, correlate(): lagged = lax.map(one_block, blocks)  18.4 us
    broadcast_in_dim x1, other arithmetic, local(): return jnp.stack(results)[:, None, None]  13.8 us
    slice x16, local copies, waits for them, and re-layouts, one_block(): slab_spec[None, :, 0, :]  13 us
    another operation x2, local copies, waits for them, and re-layouts  8.57 us
  transfers between devices with their start and end apart: 4, of which 2 were waited for; matrix products, arithmetic and copies ran while one was open for 8% of the time, Pallas kernels for 0%

profile of v1, /device:TPU:0, one launch (start us, length us, event | category | flops | bytes accessed | tf_op | source)
XLA Modules:
  0.0 299.8 jit_solution(6217098043048838610)
XLA Ops:
  0.0 2.4 multiply_reduce_fusion.1
  2.4 2.6 broadcast_multiply_fusion
  5.0 5.1 %collective-permute-start.2 = (f32[128,2,1024]{2,1,0:T(2,128)}, f32[128,2,1024]{2,1,0:T(2,128)}, u32[]{:S(2)}, u32[]{:S(2)}) collective-permute-start(f32[128,2,1024]{2,1,0:T(2,128)} %broadcast_multiply_fusion), channel_id=1, source_target_pairs={{1,0},{2,1},{3,2},{0,3},{5,4},{6,5},{7,6},{4,7},{9,8},{10,9},{11,1... | collective-permute-start | bytes 3145736 | tf_op jit(solution)/shard_map/ppermute | solution.py:82
  11.4 2.3 multiply_reduce_fusion
  13.7 1.7 multiply_multiply_fusion
  15.4 1.7 gather_fusion.1
  17.1 39.1 %collective-permute-done = f32[128,2,1024]{2,1,0:T(2,128)} collective-permute-done((f32[128,2,1024]{2,1,0:T(2,128)}, f32[128,2,1024]{2,1,0:T(2,128)}, u32[]{:S(2)}, u32[]{:S(2)}) %collective-permute-start) | collective-permute-done | bytes 1048608 | tf_op jit(solution)/shard_map/ppermute | solution.py:80
  60.9 21.4 %collective-permute-done.1 = f32[128,2,1024]{2,1,0:T(2,128)} collective-permute-done((f32[128,2,1024]{2,1,0:T(2,128)}, f32[128,2,1024]{2,1,0:T(2,128)}, u32[]{:S(2)}, u32[]{:S(2)}) %collective-permute-start.1) | collective-permute-done | bytes 1048608 | tf_op jit(solution)/shard_map/ppermute | solution.py:80
  82.4 5.2 %pad_maximum_fusion = f32[4,128,2,1024]{3,2,1,0:T(2,128)} fusion(f32[1,128,2,1024]{3,2,1,0:T(2,128)} %bitcast.3, f32[1,128,2,1024]{3,2,1,0:T(2,128)S(1)} %fusion.64, f32[1,128,2,1024]{3,2,1,0:T(2,128)} %bitcast.1, f32[1,128,2,1024]{3,2,1,0:T(2,128)} %bitcast), kind=kLoop, calls=%fused_computation.77 | loop fusion | flops 3145728 | bytes 8388608 | tf_op jit(solution)/shard_map/stack | solution.py:83
  87.6 8.4 %gather_fusion = f32[4,128,2,1024]{3,2,1,0:T(2,128)} fusion(f32[4,128,2,1024]{3,2,1,0:T(2,128)} %pad_maximum_fusion, s32[1024]{0:T(1024)S(1)} %pad_clamp_fusion.1), kind=kCustom, calls=%fused_computation | custom fusion | bytes 8388624 | tf_op jit(solution)/shard_map/gather | solution.py:85
  95.9 3.2 %constant_dynamic-slice_fusion.1 = (f32[128,2,1024]{2,1,0:T(2,128)S(1)}, f32[128,2,1024]{2,1,0:T(2,128)}) fusion(f32[512,2,1024]{2,1,0:T(2,128)} %bitcast.100, s32[]{:T(128)S(6)} %select_n.69, s32[]{:T(128)S(6)} %select_n.74), kind=kLoop, calls=%fused_computation.93 | loop fusion | bytes 4194312 | tf_op jit(solution)/shard_map/dynamic_slice | solution.py:93
  99.1 4.3 %broadcast.154.clone = bf16[8,16,128,256]{3,2,1,0:T(8,128)(2,1)} broadcast(bf16[]{:T(256)} %constant.84.clone.1), dimensions={} | broadcast | bytes 8388610 | tf_op jit(solution)/shard_map/broadcast.10
  103.4 92.7 %while.25 = (s32[]{:T(128)}, bf16[8,16,128,256]{3,2,1,0:T(8,128)(2,1)}, f32[8,16,2,1024]{3,2,1,0:T(2,128)}, f32[128,2,1024]{2,1,0:T(2,128)S(1)}, s32[128]{0:T(128)S(1)}, /*index=5*/s32[]{:T(128)}) while((s32[]{:T(128)}, bf16[8,16,128,256]{3,2,1,0:T(8,128)(2,1)}, f32[8,16,2,1024]{3,2,1,0:T(2,128)}, ...), condition=%wide.region_5.6_spmd.clone.clone, body=%wide.region_4.5_spmd.clone.clone.sunk | while | flops 1097990144 | bytes 28181588 | solution.py:60
  105.5 2.7 subtract_convert_fusion.7
  108.2 2.9 fusion.84
  111.1 2.8 add_convert_fusion.7
  117.1 2.7 subtract_convert_fusion.7
  119.8 2.9 fusion.84
  122.6 2.8 add_convert_fusion.7
  128.7 2.7 subtract_convert_fusion.7
  131.4 2.9 fusion.84
  134.2 2.8 add_convert_fusion.7
  140.3 2.7 subtract_convert_fusion.7
  142.9 2.9 fusion.84
  145.8 2.8 add_convert_fusion.7
  151.9 2.7 subtract_convert_fusion.7
  154.5 2.9 fusion.84
  157.4 2.8 add_convert_fusion.7
  163.4 2.7 subtract_convert_fusion.7
  166.1 2.9 fusion.84
  169.0 2.8 add_convert_fusion.7
  175.0 2.7 subtract_convert_fusion.7
  177.7 2.9 fusion.84
  180.6 2.8 add_convert_fusion.7
  186.6 2.7 subtract_convert_fusion.7
  189.3 2.9 fusion.84
  192.2 2.8 add_convert_fusion.7
  196.2 4.3 %broadcast.154.clone.1 = bf16[8,16,128,256]{3,2,1,0:T(8,128)(2,1)} broadcast(bf16[]{:T(256)} %constant.84.clone.1), dimensions={} | broadcast | bytes 8388610 | tf_op jit(solution)/shard_map/broadcast.10
  200.4 85.5 %while.24 = (s32[]{:T(128)}, bf16[8,16,128,256]{3,2,1,0:T(8,128)(2,1)}, f32[8,16,2,1024]{3,2,1,0:T(2,128)S(1)}, f32[128,2,1024]{2,1,0:T(2,128)S(1)}, s32[128]{0:T(128)S(1)}, /*index=5*/s32[]{:T(128)}) while((s32[]{:T(128)}, bf16[8,16,128,256]{3,2,1,0:T(8,128)(2,1)}, f32[8,16,2,1024]{3,2,1,0:T(2,128)S(1)}, ...), condition=%wide.region_3.4_spmd.clone.clone, body=%wide.region_2.3_spmd.clone.clone.sunk | while | flops 1097990144 | bytes 28181588 | solution.py:60
  201.6 2.7 subtract_convert_fusion.6
  204.3 2.9 fusion.79
  207.2 2.8 add_convert_fusion.6
  212.4 2.7 subtract_convert_fusion.6
  215.0 2.9 fusion.79
  217.9 2.8 add_convert_fusion.6
  223.0 2.7 subtract_convert_fusion.6
  225.7 2.9 fusion.79
  228.6 2.8 add_convert_fusion.6
  233.7 2.7 subtract_convert_fusion.6
  236.4 2.9 fusion.79
  239.2 2.8 add_convert_fusion.6
  244.4 2.7 subtract_convert_fusion.6
  247.1 2.9 fusion.79
  249.9 2.8 add_convert_fusion.6
  255.1 2.7 subtract_convert_fusion.6
  257.8 2.9 fusion.79
  260.6 2.8 add_convert_fusion.6
  265.8 2.7 subtract_convert_fusion.6
  268.4 2.9 fusion.79
  271.3 2.8 add_convert_fusion.6
  276.4 2.7 subtract_convert_fusion.6
  279.1 2.9 fusion.79
  282.0 2.8 add_convert_fusion.6
  285.9 13.8 %maximum_bitcast_fusion = bf16[2,1,1,128,128,256]{5,4,3,2,1,0:T(8,128)(2,1)} fusion(bf16[1,128,128,256]{3,2,1,0:T(8,128)(2,1)} %bitcast.95, bf16[1,128,128,256]{3,2,1,0:T(8,128)(2,1)} %bitcast.94), kind=kLoop, calls=%fused_computation.76 | loop fusion | flops 8388608 | bytes 33554432 | tf_op jit(solution)/shard_map/broadcast_in_dim | solution.py:95
  (122 shorter events, 48.7 us)
Async XLA Ops:
  0.0 58.4 %copy-start = (s32[2,8]{1,0:T(2,128)S(1)}, s32[2,8]{1,0:T(2,128)}, u32[]{:S(2)}) copy-start(s32[2,8]{1,0:T(2,128)} %param.13) | copy-start | bytes 196
  0.0 60.5 %copy-start.2 = (f32[128,2,1024]{2,1,0:T(2,128)S(1)}, f32[128,2,1024]{2,1,0:T(2,128)}, u32[]{:S(2)}) copy-start(f32[128,2,1024]{2,1,0:T(2,128)} %param.10) | copy-start | bytes 3145732
  0.0 17.1 %copy-start.3 = (s32[1,128]{1,0:T(1,128)S(1)}, s32[1,128]{1,0:T(1,128)}, u32[]{:S(2)}) copy-start(s32[1,128]{1,0:T(1,128)} %param.12) | copy-start | bytes 1540
  5.0 55.9 %collective-permute-start.2 = (f32[128,2,1024]{2,1,0:T(2,128)}, f32[128,2,1024]{2,1,0:T(2,128)}, u32[]{:S(2)}, u32[]{:S(2)}) collective-permute-start(f32[128,2,1024]{2,1,0:T(2,128)} %broadcast_multiply_fusion), channel_id=1, source_target_pairs={{1,0},{2,1},{3,2},{0,3},{5,4},{6,5},{7,6},{4,7},{9,8},{10,9},{11,1... | collective-permute-start | bytes 3145736 | tf_op jit(solution)/shard_map/ppermute | solution.py:82
  10.1 46.1 %collective-permute-start = (f32[128,2,1024]{2,1,0:T(2,128)}, f32[128,2,1024]{2,1,0:T(2,128)}, u32[]{:S(2)}, u32[]{:S(2)}) collective-permute-start(f32[128,2,1024]{2,1,0:T(2,128)} %broadcast_multiply_fusion), channel_id=1, source_target_pairs={{0,1},{1,2},{2,3},{3,0},{4,5},{5,6},{6,7},{7,4},{8,9},{9,10},{10,1... | collective-permute-start | bytes 3145736 | tf_op jit(solution)/shard_map/ppermute | solution.py:80
  56.2 26.2 %collective-permute-start.1 = (f32[128,2,1024]{2,1,0:T(2,128)}, f32[128,2,1024]{2,1,0:T(2,128)}, u32[]{:S(2)}, u32[]{:S(2)}) collective-permute-start(f32[128,2,1024]{2,1,0:T(2,128)} %collective-permute-done), channel_id=1, source_target_pairs={{0,1},{1,2},{2,3},{3,0},{4,5},{5,6},{6,7},{7,4},{8,9},{9,10},{10,1... | collective-permute-start | bytes 3145736 | tf_op jit(solution)/shard_map/ppermute | solution.py:80
  58.4 40.8 %collective-permute-start.3 = (f32[128,2,1024]{2,1,0:T(2,128)S(1)}, f32[128,2,1024]{2,1,0:T(2,128)S(1)}, u32[]{:S(2)}, u32[]{:S(2)}) collective-permute-start(f32[128,2,1024]{2,1,0:T(2,128)S(1)} %broadcast_select_fusion), channel_id=1, source_target_pairs={{0,4},{4,8},{8,12},{12,16},{16,20},{20,24},{24,28},{28,0},{1,5},{5... | collective-permute-start | bytes 3145736 | tf_op jit(solution)/shard_map/ppermute | solution.py:20
  285.9 13.8 %copy-start.1 = (s32[2,8]{1,0:T(2,128)S(1)}, s32[2,8]{1,0:T(2,128)}, u32[]{:S(2)}) copy-start(s32[2,8]{1,0:T(2,128)} %param.13) | copy-start | bytes 196
